TPU v7x, 768 devices: a whole 4x8x12 slice. The times are simulated.
768 devices in a mesh: wave: 96 (over z, x, core), band: 8 (over y).
Axes of the slice: x: 4, y: 8, z: 12, core: 2. Of those that a mesh axis runs over, the one named last changes fastest.
Arguments:
- spectral: bfloat16 [2016, 2, 128, 1280], P('wave', None, 'band'), may hold values from -0.0059814453 to 0.0059814453
- legendre: bfloat16 [2016, 96, 1280], P('wave'), may hold values from -4 to 4
- slot_wave: int32 [2016], replicated, may hold values from 0 to 1280, as said below
- lat_points: int32 [96], P('wave'), may hold values from 20 to 5136, as said below
- level_mix: float32 [32, 32], replicated, may hold values from -1 to 1
- grid_scale: float32 [96, 6144], P('wave', 'band'), may hold values from 0.5 to 2
- gauss_w: float32 [96], replicated, may hold values from 2 to 8
Outputs:
- grid_out: float32 [128, 96, 6144], P(None, 'wave', 'band')
- spec_out: bfloat16 [2016, 2, 128, 1280], P('wave', None, 'band')
Inputs may be any that keep to these rules, and one draw needn't show every extreme that they name: `slot_wave`: every wavenumber 0 to 1279 is held by exactly one slot; all other slots hold 1280; some index of wave has all 21 of its slots holding wavenumbers. `lat_points`: each value is 20 + 4 i for a latitude row i from 0 to 1279; some latitude has 5136 points.
All inputs are finite; a program needn't handle non-finite values.
Results may differ from a plain program's by a relative error of at most 0.0062.
Values may be sent and summed in bfloat16 or wider, within the bound.
No kernel may reach another device: no remote copies, remote signals or barrier semaphores. Data moves between devices by JAX's collectives and lax.ppermute only.
A program may use at most 64 MiB of HBM per device.

v0:
```python
import math

import jax
import jax.numpy as jnp
from jax import lax
from jax.sharding import PartitionSpec as P

M = 1280
NLEV = 32


TWO_PI = 2.0 * math.pi


def trig_table(wave_ids, points, lon_first, lon_width):
    lon_index = lon_first + jnp.arange(lon_width, dtype=jnp.int32)
    turn_index = wave_ids[None, :, None] * lon_index[None, None, :] % points[:, None, None]
    angle_rad = (
        turn_index.astype(jnp.float32) * (TWO_PI / points.astype(jnp.float32))[:, None, None]
    )
    return jnp.stack([jnp.cos(angle_rad), jnp.sin(angle_rad)], axis=2)


def valid_waves(wave_ids, points):
    return ((wave_ids[None, :] < M) & (2 * wave_ids[None, :] < points[:, None])).astype(jnp.float32)


def lon_mask(points, lon_first, lon_width):
    lon_index = lon_first + jnp.arange(lon_width, dtype=jnp.int32)
    return (lon_index[None, :] < points[:, None]).astype(jnp.float32)


def inverse_terms(four_coef, wave_ids, points, lon_first, lon_width):
    valid_wave = valid_waves(wave_ids, points)
    doubled = jnp.where(wave_ids == 0, 1.0, 2.0).astype(jnp.float32)
    sign_pair = jnp.array([1.0, -1.0], jnp.float32)
    factor = (valid_wave * doubled[None, :])[:, :, None] * sign_pair
    weighted = four_coef.astype(jnp.float32) * jnp.transpose(factor, (1, 2, 0))[:, :, None, :]
    trig_tab = trig_table(wave_ids, points, lon_first, lon_width)
    grid_rows = jnp.einsum("scfa,ascj->faj", weighted, trig_tab, precision=lax.Precision.HIGHEST)
    return grid_rows * lon_mask(points, lon_first, lon_width)[None]


def direct_terms(grid_rows, wave_ids, points, lon_first, lon_width):
    valid_wave = valid_waves(wave_ids, points)
    sign_pair = jnp.array([1.0, -1.0], jnp.float32)
    trig_tab = trig_table(wave_ids, points, lon_first, lon_width)
    masked_rows = grid_rows * lon_mask(points, lon_first, lon_width)[None]
    summed = jnp.einsum("faj,ascj->fsca", masked_rows, trig_tab, precision=lax.Precision.HIGHEST)
    factor = valid_wave[:, :, None] * sign_pair / points.astype(jnp.float32)[:, None, None]
    return summed * jnp.transpose(factor, (1, 2, 0))[None]


def mix_levels(grid_rows, level_mix, grid_scale):
    fields, lats, lons = grid_rows.shape
    stacked = grid_rows.reshape(fields // NLEV, NLEV, lats, lons)
    mixed_grid = jnp.einsum("ik,bkaj->biaj", level_mix, stacked, precision=lax.Precision.HIGHEST)
    return mixed_grid.reshape(fields, lats, lons) * grid_scale[None]


def body(spectral, legendre, slot_wave, lat_points, level_mix, grid_scale, gauss_w):
    slot_count = spectral.shape[0]
    wave_here = lax.dynamic_slice_in_dim(slot_wave, lax.axis_index("wave") * slot_count, slot_count)
    degree = jnp.arange(spectral.shape[3], dtype=jnp.int32)
    keep_mask = degree[None, :] >= wave_here[:, None]
    masked = jnp.where(keep_mask[:, None, None, :], spectral, jnp.zeros((), jnp.bfloat16))
    four_coef = jnp.einsum(
        "scfn,sln->scfl", masked, legendre, preferred_element_type=jnp.float32
    ).astype(jnp.bfloat16)
    fourier = lax.all_to_all(four_coef, "wave", split_axis=3, concat_axis=0, tiled=True)
    lon_width = grid_scale.shape[1]
    lon_first = lax.axis_index("band") * lon_width
    grid_rows = inverse_terms(
        lax.all_gather(fourier, "band", axis=2, tiled=True),
        slot_wave,
        lat_points,
        lon_first,
        lon_width,
    )
    mixed_grid = mix_levels(grid_rows, level_mix, grid_scale)
    back_coef = lax.psum_scatter(
        direct_terms(mixed_grid, slot_wave, lat_points, lon_first, lon_width),
        "band",
        scatter_dimension=0,
        tiled=True,
    )
    fourier_back = lax.all_to_all(
        back_coef.astype(jnp.bfloat16), "wave", split_axis=1, concat_axis=3, tiled=True
    )
    fourier_back = lax.optimization_barrier(fourier_back)
    weighted = (fourier_back.astype(jnp.float32) * gauss_w[None, None, None, :]).astype(
        jnp.bfloat16
    )
    summed = jnp.einsum("fscl,sln->scfn", weighted, legendre, preferred_element_type=jnp.float32)
    spec_out = jnp.where(keep_mask[:, None, None, :], summed, 0.0).astype(jnp.bfloat16)
    return (grid_rows, spec_out)


def solution(mesh):
    placed = (
        P("wave", None, "band", None),
        P("wave", None, None),
        P(),
        P("wave"),
        P(),
        P("wave", "band"),
        P(),
    )
    return jax.shard_map(
        body,
        mesh=mesh,
        in_specs=placed,
        out_specs=(P(None, "wave", "band"), P("wave", None, "band", None)),
        check_vma=False,
    )
```

profile of v0, /device:TPU:1, one launch (start us, length us, event | category | flops | bytes accessed | tf_op | source)
XLA Modules:
  0.0 278.9 jit_solution(17517977535489881927)
XLA Ops:
  0.6 0.0 copy-start
  0.6 0.0 copy-start.3
  0.7 0.0 copy-start.4
  0.7 0.8 dynamic_slice.3
  1.5 0.1 iota_compare_fusion
  1.6 0.0 copy-start.1
  1.6 0.6 copy-done.1
  2.2 4.9 %fusion.35 = bf16[21,2,16,96]{3,2,1,0:T(8,128)(2,1)S(1)} fusion(bf16[21,96,1280]{2,1,0:T(8,128)(2,1)} %param.12, bf16[21,2,16,1280]{3,2,1,0:T(8,128)(2,1)} %param.11, pred[21,1280]{1,0:T(8,128)(4,1)S(1)} %iota_compare_fusion), kind=kOutput, calls=%fused_computation.30 | convolution fusion | flops 166075392 | bytes 7037184 | tf_op jit(solution)/shard_map/scfn,sln->scfl/dot_general | solution.py:67
  7.1 1.2 copy.34
  8.3 1.7 reshape.286
  10.0 20.0 %all-to-all-start = ((bf16[96,2,336]{2,1,0:T(2,128)(2,1)}), bf16[96,2,336]{2,1,0:T(2,128)(2,1)S(1)}, u32[]{:S(2)}, u32[]{:S(2)}) async-start(bf16[96,2,336]{2,1,0:T(2,128)(2,1)} %reshape.286), calls=%async_computation | async-start | bytes 294912 | tf_op jit(solution)/shard_map/all_to_all | solution.py:70
  30.7 0.0 copy-done.3
  30.8 0.0 copy-done.4
  30.9 1.3 dynamic-slice
  32.8 0.0 copy-start.5
  32.8 84.3 %cosine_bitcast_fusion = (f32[1,2016,1,768]{3,1,2,0:T(8,128)}, f32[1,2016,1,768]{3,1,2,0:T(8,128)}) fusion(s32[]{:T(128)} %bitcast.1, f32[]{:T(128)} %bitcast.3, s32[768]{0:T(1024)S(1)} %iota_add_fusion, s32[2016]{0:T(1024)S(1)} %copy-done.3, pred[]{:T(512)} %bitcast.2), kind=kLoop, calls=%fused_computation.7 | loop fusion | flops 15482880 | bytes 12397449 | tf_op jit(solution)/shard_map/stack | solution.py:21
  117.1 0.0 copy-done.5
  117.1 0.1 multiply_divide_fusion
  117.2 0.0 all-to-all-done
  117.2 1.1 reshape.287
  118.3 0.1 bitcast_bitcast_fusion
  118.4 0.3 copy.35
  118.7 0.9 all_to_all.29
  119.7 0.0 slice-start.2
  119.7 23.3 %all_gather.3 = bf16[2016,2,128,1]{0,2,1,3:T(8,128)(2,1)S(1)} all-gather(bf16[2016,2,16,1]{0,2,1,3:T(8,128)(2,1)S(1)} %all_to_all.29), channel_id=1, replica_groups=mesh['wave'=96,'band'=8] {'band'}, dimensions={2}, use_global_device_ids=true | all-gather | bytes 1161216 | tf_op jit(solution)/shard_map/all_gather | solution.py:74
  143.0 12.6 %fusion.32 = f32[1,768,128]{1,2,0:T(8,128)S(1)} fusion(bf16[2016,2,128,1]{0,2,1,3:T(8,128)(2,1)S(1)} %all_gather.3, f32[1,2016,1,768]{3,1,2,0:T(8,128)} %get-tuple-element.14, f32[1,2016,1,768]{3,1,2,0:T(8,128)} %get-tuple-element.13, f32[2016,2]{0,1:T(2,128)S(1)} %get-tuple-element.16, f32[768]{0:T(1024)S(1)} %compare_convert_fusion), kind=kOutput, calls=%fused_computation.29 | convolution fusion | flops 4760567808 | bytes 13830912 | tf_op jit(solution)/shard_map/scfa,ascj->faj/dot_general | solution.py:40
  155.7 0.0 copy-done
  155.7 0.5 fusion.48
  156.2 0.0 slice-done
  156.2 0.0 slice-done.2
  156.2 0.0 slice-done.1
  156.2 0.0 slice-done.3
  156.2 11.2 %fusion.23 = f32[128,2016,2,1]{0,1,2,3:T(8,128)} fusion(f32[1,2016,1,768]{3,1,2,0:T(8,128)S(1)} %bitcast.104, f32[1,2016,1,768]{3,1,2,0:T(8,128)S(1)} %bitcast.102, f32[2016,2]{0,1:T(2,128)S(1)} %get-tuple-element.15, f32[128,1,1,1,1,1,768]{6,0,5,4,3,2,1:T(8,128)S(1)} %bitcast.110, f32[768]{0:T(1024)S(1)} %compare_convert_fusion, f32[768]{0:T(1024)S(1)} %reduce), kind=kOutput, calls=%fused_computation.22 | convolution fusion | flops 4760150016 | bytes 14866176 | tf_op jit(solution)/shard_map/faj,ascj->fsca/dot_general | solution.py:49
  167.4 2.9 %copy.37 = f32[128,2016,2,1]{1,2,3,0:T(2,128)S(1)} copy(f32[128,2016,2,1]{0,1,2,3:T(8,128)} %fusion.23) | data formatting | bytes 4128768 | tf_op jit(solution)/shard_map/mul | solution.py:51
  170.4 53.6 %all-reduce.2 = bf16[128,2016,2,1]{1,2,3,0:T(2,128)(2,1)S(1)} all-reduce(f32[128,2016,2,1]{1,2,3,0:T(2,128)S(1)} %copy.37), channel_id=2, replica_groups=mesh['wave'=96,'band'=8] {'band'}, use_global_device_ids=true, to_apply=%region_0.2.clone | all-reduce | flops 516096 | bytes 3096576
  224.0 0.0 copy-start.2
  224.0 0.0 copy-start.6
  224.0 0.1 dynamic-slice_convert_fusion
  224.1 1.2 copy.38
  225.3 1.6 reshape.288
  226.9 30.8 %all-to-all-start.1 = ((bf16[96,2,336]{2,1,0:T(2,128)(2,1)}), bf16[96,2,336]{2,1,0:T(2,128)(2,1)S(1)}, u32[]{:S(2)}, u32[]{:S(2)}) async-start(bf16[96,2,336]{2,1,0:T(2,128)(2,1)} %reshape.288), calls=%async_computation.1 | async-start | bytes 294912 | tf_op jit(solution)/shard_map/all_to_all | solution.py:87
  257.7 1.2 copy.41
  258.9 13.9 %all-to-all-done.1 = bf16[96,2,336]{2,1,0:T(2,128)(2,1)S(1)} async-done(((bf16[96,2,336]{2,1,0:T(2,128)(2,1)}), bf16[96,2,336]{2,1,0:T(2,128)(2,1)S(1)}, u32[]{:S(2)}, u32[]{:S(2)}) %all-to-all-start.1) | async-done | bytes 129056 | tf_op jit(solution)/shard_map/all_to_all | solution.py:87
  272.8 0.9 reshape.289
  273.7 0.7 copy.40
  274.4 0.0 copy-done.2
  274.4 0.0 copy-done.6
  274.4 4.5 %fusion.18 = bf16[21,2,16,1280]{3,2,1,0:T(8,128)(2,1)} fusion(bf16[21,96,1280]{2,1,0:T(8,128)(2,1)} %param.12, pred[21,1280]{1,0:T(8,128)(4,1)S(1)} %copy-done.2, bf16[16,21,2,96]{3,0,2,1:T(8,128)(2,1)S(1)} %bitcast.111, f32[96]{0:T(128)S(1)} %copy-done.6), kind=kOutput, calls=%fused_computation.19 | convolution fusion | flops 167064576 | bytes 7037568 | tf_op jit(solution)/shard_map/fscl,sln->scfn/dot_general | solution.py:94
  (10 shorter events, 0.0 us)
Async XLA Ops:
  0.6 155.1 %copy-start = (f32[32,32]{1,0:T(8,128)S(1)}, f32[32,32]{1,0:T(8,128)}, u32[]{:S(2)}) copy-start(f32[32,32]{1,0:T(8,128)} %param.15) | copy-start | bytes 12292
  0.6 30.1 %copy-start.3 = (s32[2016]{0:T(1024)S(1)}, s32[2016]{0:T(1024)}, u32[]{:S(2)}) copy-start(s32[2016]{0:T(1024)} %param.13) | copy-start | bytes 24196
  0.7 30.2 %copy-start.4 = (f32[1,768]{1,0:T(1,128)S(1)}, f32[1,768]{1,0:T(1,128)}, u32[]{:S(2)}) copy-start(f32[1,768]{1,0:T(1,128)} %param.16) | copy-start | bytes 9220
  1.6 0.6 copy-start.1
  10.0 107.2 %all-to-all-start = ((bf16[96,2,336]{2,1,0:T(2,128)(2,1)}), bf16[96,2,336]{2,1,0:T(2,128)(2,1)S(1)}, u32[]{:S(2)}, u32[]{:S(2)}) async-start(bf16[96,2,336]{2,1,0:T(2,128)(2,1)} %reshape.286), calls=%async_computation | async-start | bytes 294912 | tf_op jit(solution)/shard_map/all_to_all | solution.py:70
  32.8 84.3 %copy-start.5 = (f32[2]{0:T(128)S(1)}, f32[2]{0:T(128)}, u32[]{:S(2)}) copy-start(f32[2]{0:T(128)} %constant.40.clone) | copy-start | bytes 28
  119.7 36.5 %slice-start = ((s8[6193152]{0:T(1024)(128)(4,1)}), s8[4194304]{0:T(1024)(128)(4,1)S(1)}, s32[]{:S(2)}) async-start(s8[6193152]{0:T(1024)(128)(4,1)} %bitcast.101), calls=%async_computation.2 | async-start | bytes 8388608
  119.7 36.5 %slice-start.2 = ((s8[6193152]{0:T(1024)(128)(4,1)}), s8[4194304]{0:T(1024)(128)(4,1)S(1)}, s32[]{:S(2)}) async-start(s8[6193152]{0:T(1024)(128)(4,1)} %bitcast.103), calls=%async_computation.4 | async-start | bytes 8388608
  143.0 13.1 %slice-start.1 = ((s8[6193152]{0:T(1024)(128)(4,1)}), s8[1998848]{0:T(1024)(128)(4,1)S(1)}, s32[]{:S(2)}) async-start(s8[6193152]{0:T(1024)(128)(4,1)} %bitcast.101), calls=%async_computation.3 | async-start | bytes 3997696
  143.0 13.1 %slice-start.3 = ((s8[6193152]{0:T(1024)(128)(4,1)}), s8[1998848]{0:T(1024)(128)(4,1)S(1)}, s32[]{:S(2)}) async-start(s8[6193152]{0:T(1024)(128)(4,1)} %bitcast.103), calls=%async_computation.5 | async-start | bytes 3997696
  224.0 50.5 %copy-start.2 = (pred[21,1280]{1,0:T(8,128)(4,1)S(1)}, pred[21,1280]{1,0:T(8,128)(4,1)}, u32[]{:S(2)}) copy-start(pred[21,1280]{1,0:T(8,128)(4,1)} %copy-done.1) | copy-start | bytes 80644
  224.0 50.5 %copy-start.6 = (f32[96]{0:T(128)S(1)}, f32[96]{0:T(128)}, u32[]{:S(2)}) copy-start(f32[96]{0:T(128)} %param.17) | copy-start | bytes 1156
  226.9 45.9 %all-to-all-start.1 = ((bf16[96,2,336]{2,1,0:T(2,128)(2,1)}), bf16[96,2,336]{2,1,0:T(2,128)(2,1)S(1)}, u32[]{:S(2)}, u32[]{:S(2)}) async-start(bf16[96,2,336]{2,1,0:T(2,128)(2,1)} %reshape.288), calls=%async_computation.1 | async-start | bytes 294912 | tf_op jit(solution)/shard_map/all_to_all | solution.py:87
where the time goes:
time: 279 us
  other arithmetic  84.5 us (30%)
  blocking collectives  76.9 us (28%)
  starting transfers between devices  50.8 us (18%)
  matrix products  33.7 us (12%)
  local copies, waits for them, and re-layouts  16.8 us (6%)
  waiting for transfers between devices  13.9 us (5%)
    another operation x1, other arithmetic, trig_table(): return jnp.stack([jnp.cos(angle_rad), jnp.sin(angle_rad)], axis=2)  84.3 us
    unnamed x1, blocking collectives  53.6 us
    all_to_all x1, starting transfers between devices, body(): lax.all_to_all(back_coef.astype(jnp.bfloat16), 'wave', split_axis=1, conc...  30.8 us
    all_gather x1, blocking collectives, body(): lax.all_gather(fourier, 'band', axis=2, tiled=True)  23.3 us
    all_to_all x1, starting transfers between devices, body(): lax.all_to_all(four_coef, 'wave', split_axis=3, concat_axis=0, tiled=True)  20 us
    all_to_all x1, waiting for transfers between devices, body(): lax.all_to_all(back_coef.astype(jnp.bfloat16), 'wave', split_axis=1, conc...  13.9 us
    dot_general x1, matrix products, inverse_terms(): jnp.einsum('scfa,ascj->faj', weighted, trig_tab, precision=lax.Precision....  12.6 us
    dot_general x1, matrix products, direct_terms(): jnp.einsum('faj,ascj->fsca', masked_rows, trig_tab, precision=lax.Precisi...  11.2 us
  transfers between devices with their start and end apart: 2, of which 1 were waited for; matrix products, arithmetic and copies ran while one was open for 31% of the time, Pallas kernels for 0%

commit v1 on v0

v1 whole, which is shorter than its diff:
```python
import math

import jax
import jax.numpy as jnp
from jax import lax
from jax.experimental import pallas as pl
from jax.experimental.pallas import tpu as pltpu
from jax.sharding import PartitionSpec as P


M = 1280
LAT = 96
GROUP = 3
ROWS = 8
KPAD = GROUP * LAT * ROWS
QPAD = 1408
LONS = 6144
TWO_PI = 2.0 * math.pi
F32 = jnp.float32
BF16 = jnp.bfloat16

NT = (((1,), (1,)), ((), ()))


def spectral_copies(spec_ref, leg_ref, spec_buf, leg_buf, sems):
    copies = []
    for step in range(leg_ref.shape[0] // GROUP):
        at = pl.ds(step * GROUP, GROUP)
        copies.append(
            (
                pltpu.make_async_copy(spec_ref.at[at], spec_buf.at[at], sems.at[0, step]),
                pltpu.make_async_copy(leg_ref.at[at], leg_buf.at[at], sems.at[1, step]),
            )
        )
    return copies


def legendre_inverse_kernel(base_ref, wave_ref, spec_ref, leg_ref, out_ref, spec_buf, leg_buf, acc_ref, sems):
    copies = spectral_copies(spec_ref, leg_ref, spec_buf, leg_buf, sems)
    for pair in copies:
        for copy in pair:
            copy.start()
    acc_ref[pl.ds(ROWS - 1, LAT, stride=ROWS), :] = jnp.zeros((LAT, 128), F32)
    degree = lax.broadcasted_iota(jnp.int32, (32, M), 1)
    for step, pair in enumerate(copies):
        for copy in pair:
            copy.wait()
        parts = []
        for k in range(step * GROUP, step * GROUP + GROUP):
            wave = wave_ref[base_ref[0] + k]
            coef = jnp.where(degree >= wave, spec_buf[k].astype(F32), 0.0).astype(BF16)
            parts.append(lax.dot_general(leg_buf[k], coef, NT, preferred_element_type=F32))
        parts.append(jnp.zeros((LAT, 32), F32))
        acc_ref[pl.ds(step, LAT, stride=ROWS), :] = jnp.concatenate(parts, axis=1)
    out_ref[...] = acc_ref[...].astype(BF16)


def legendre_inverse(base, slot_wave, spectral, legendre):
    slots = spectral.shape[0]
    smem = pl.BlockSpec(memory_space=pltpu.SMEM)
    hbm = pl.BlockSpec(memory_space=pl.ANY)
    return pl.pallas_call(
        legendre_inverse_kernel,
        in_specs=[smem, smem, hbm, hbm],
        out_specs=pl.BlockSpec(memory_space=pltpu.VMEM),
        out_shape=jax.ShapeDtypeStruct((LAT * ROWS, 128), BF16),
        scratch_shapes=[
            pltpu.VMEM((slots, 32, M), BF16),
            pltpu.VMEM((slots, LAT, M), BF16),
            pltpu.VMEM((LAT * ROWS, 128), F32),
            pltpu.SemaphoreType.DMA((2, slots // GROUP)),
        ],
        name="legendre_inverse",
    )(base, slot_wave, spectral.reshape(slots, 32, M), legendre)


def legendre_direct_kernel(base_ref, wave_ref, coef_ref, leg_ref, gauss_ref, out_ref, leg_buf, out_buf, acc_ref, sems):
    steps = leg_ref.shape[0] // GROUP
    loads = []
    stores = []
    for step in range(steps):
        at = pl.ds(step * GROUP, GROUP)
        loads.append(pltpu.make_async_copy(leg_ref.at[at], leg_buf.at[at], sems.at[0, step]))
        stores.append(pltpu.make_async_copy(out_buf.at[at], out_ref.at[at], sems.at[1, step]))
    for copy in loads:
        copy.start()
    acc_ref[pl.ds(0, LAT * ROWS), :] = coef_ref[...].astype(F32)
    acc_ref[pl.ds(LAT * ROWS, (128 - LAT) * ROWS), :] = jnp.zeros(((128 - LAT) * ROWS, 128), F32)
    degree = lax.broadcasted_iota(jnp.int32, (32, M), 1)
    for step in range(steps):
        rows = acc_ref[pl.ds(step, 128, stride=ROWS), :]
        weighted = (rows.T[:, :LAT] * gauss_ref[...]).astype(BF16)
        loads[step].wait()
        for j in range(GROUP):
            k = step * GROUP + j
            wave = wave_ref[base_ref[0] + k]
            summed = jnp.dot(weighted[32 * j : 32 * j + 32], leg_buf[k], preferred_element_type=F32)
            out_buf[k] = jnp.where(degree >= wave, summed, 0.0).astype(BF16)
        stores[step].start()
    for copy in stores:
        copy.wait()


def legendre_direct(base, slot_wave, coef, legendre, gauss_w):
    slots = legendre.shape[0]
    smem = pl.BlockSpec(memory_space=pltpu.SMEM)
    vmem = pl.BlockSpec(memory_space=pltpu.VMEM)
    hbm = pl.BlockSpec(memory_space=pl.ANY)
    return pl.pallas_call(
        legendre_direct_kernel,
        in_specs=[smem, smem, vmem, hbm, vmem],
        out_specs=hbm,
        out_shape=jax.ShapeDtypeStruct((slots, 32, M), BF16),
        scratch_shapes=[
            pltpu.VMEM((slots, LAT, M), BF16),
            pltpu.VMEM((slots, 32, M), BF16),
            pltpu.VMEM((128 * ROWS, 128), F32),
            pltpu.SemaphoreType.DMA((2, slots // GROUP)),
        ],
        name="legendre_direct",
    )(base, slot_wave, coef, legendre, gauss_w[None, :])


def turn(product, points, inverse, quarter):
    rest = product - jnp.floor(product * inverse) * points
    rest = jnp.where(rest < 0.0, rest + points, rest)
    rest = jnp.where(rest >= points, rest - points, rest)
    quad = jnp.floor(rest * (4.0 * inverse) + 0.5)
    x = (rest - quad * quarter) * (TWO_PI * inverse)
    x2 = x * x
    s = x + x * x2 * (-1.6666654611e-1 + x2 * (8.3321608736e-3 - x2 * 1.9515295891e-4))
    c = 1.0 - 0.5 * x2 + x2 * x2 * (
        4.166664568298827e-2 + x2 * (-1.388731625493765e-3 + x2 * 2.443315711809948e-5)
    )
    swap = (quad == 1.0) | (quad == 3.0)
    cos = jnp.where(swap, s, c)
    sin = jnp.where(swap, c, s)
    cos = jnp.where((quad == 1.0) | (quad == 2.0), -cos, cos)
    sin = jnp.where((quad == 2.0) | (quad == 3.0), -sin, sin)
    return cos, sin


TROWS = 32


def table_kernel(points_ref, wave_ref, cos_ref, sin_ref, row_ref, even_ref, odd_ref):
    points_int = points_ref[0]

    def constants(rows):
        points = jnp.full((rows, 128), points_int, jnp.int32).astype(F32)
        quarter = jnp.full((rows, 128), points_int >> 2, jnp.int32).astype(F32)
        return points, 1.0 / points, quarter

    blocks = wave_ref.shape[0]
    row_ref[0] = wave_ref[...]
    row_ref[1], row_ref[2] = turn(wave_ref[...] * 128.0, *constants(blocks))
    points, inverse, quarter = constants(TROWS)
    lane = lax.broadcasted_iota(jnp.int32, (TROWS, 128), 1).astype(F32)

    def columns(i, col_ref):
        for k in range(3):
            col_ref[k] = jnp.broadcast_to(row_ref[k, pl.ds(i, 1), :], (128, 128)).T

    def fill(i, col_ref):
        for t in range(128 // TROWS):
            at = pl.ds(pl.multiple_of(i * 128 + t * TROWS, TROWS), TROWS)
            wave, step_cos, step_sin = (col_ref[k, t * TROWS : (t + 1) * TROWS, :] for k in range(3))
            cos, sin = turn(wave * lane, points, inverse, quarter)
            twice = 2.0 * step_cos
            last = cos * step_cos + sin * step_sin, sin * step_cos - cos * step_sin
            for u in range(QPAD // 128):
                cos_ref[at, 128 * u : 128 * u + 128] = cos.astype(BF16)
                sin_ref[at, 128 * u : 128 * u + 128] = sin.astype(BF16)
                following = twice * cos - last[0], twice * sin - last[1]
                last = cos, sin
                cos, sin = following

    columns(0, even_ref)

    def pair(p, carry):
        columns(2 * p + 1, odd_ref)
        fill(2 * p, even_ref)
        columns(jnp.minimum(2 * p + 2, blocks - 1), even_ref)
        fill(2 * p + 1, odd_ref)
        return carry

    lax.fori_loop(0, blocks // 2, pair, 0)


def trig_tables(points, wave_rows):
    vmem = pl.BlockSpec(memory_space=pltpu.VMEM)
    shape = jax.ShapeDtypeStruct((KPAD, QPAD), BF16)
    return pl.pallas_call(
        table_kernel,
        in_specs=[pl.BlockSpec(memory_space=pltpu.SMEM), vmem],
        out_specs=[vmem, vmem],
        out_shape=[shape, shape],
        scratch_shapes=[
            pltpu.VMEM((3,) + wave_rows.shape, F32),
            pltpu.VMEM((3, 128, 128), F32),
            pltpu.VMEM((3, 128, 128), F32),
        ],
        compiler_params=pltpu.CompilerParams(vmem_limit_bytes=8 << 20),
        name="tables",
    )(points, wave_rows)


def coefficients(message):
    turned = message.astype(F32).T
    real = jnp.concatenate([turned[32 * k : 32 * k + 16] for k in range(GROUP)], axis=1)
    imag = jnp.concatenate([turned[32 * k + 16 : 32 * k + 32] for k in range(GROUP)], axis=1)
    return real, imag


def classes(wave, points_int, scale):
    valid = (wave < M) & (2 * wave < points_int)
    kind = wave & 3
    return [jnp.where(valid & (kind == k), scale, 0.0) for k in range(4)]


def inverse_quarters(real, imag, wave, points_int, cos_ref, sin_ref):
    doubled = jnp.where(wave == 0, 1.0, 2.0)
    e0, e1, e2, e3 = classes(wave, points_int, doubled)
    odd = e1 + e3
    turned = e1 - e3
    left_cos = jnp.concatenate([real * e0, real * e2, real * odd, imag * turned], axis=0).astype(BF16)
    left_sin = jnp.concatenate([imag * -e0, imag * -e2, imag * -odd, real * turned], axis=0).astype(BF16)
    sums = jnp.dot(left_cos, cos_ref[...], preferred_element_type=F32)
    sums += jnp.dot(left_sin, sin_ref[...], preferred_element_type=F32)
    even = sums[0:16] + sums[16:32]
    odds = sums[0:16] - sums[16:32]
    return even + sums[32:48], odds - sums[48:64], even - sums[32:48], odds + sums[48:64]


def grid_kernel(points_ref, wave_ref, own_ref, cos_ref, sin_ref, out_ref, line_ref):
    points_int = points_ref[0]
    quarter = points_int >> 2
    real, imag = coefficients(own_ref[...])
    quarters = inverse_quarters(real, imag, wave_ref[...], points_int, cos_ref, sin_ref)
    line_ref[...] = jnp.zeros_like(line_ref)
    keep = lax.broadcasted_iota(jnp.int32, (16, QPAD), 1) < quarter
    for t in range(4):
        part = jnp.where(keep, quarters[t], 0.0)
        part = jnp.concatenate([part, jnp.zeros((16, 128), F32)], axis=1)
        if t == 0:
            line_ref[:, : QPAD + 128] += part
        else:
            first = quarter * t
            part = pltpu.roll(part, first & 127, 1)
            at = pl.ds(pl.multiple_of((first >> 7) * 128, 128), QPAD + 128)
            line_ref[:, at] += part
    bands, _, width = out_ref.shape
    for k in range(bands):
        out_ref[k] = line_ref[:, k * width : (k + 1) * width].astype(BF16)


def grid_rows(points, wave, own, cos, sin, bands):
    vmem = pl.BlockSpec(memory_space=pltpu.VMEM)
    return pl.pallas_call(
        grid_kernel,
        in_specs=[pl.BlockSpec(memory_space=pltpu.SMEM)] + [vmem] * 4,
        out_specs=vmem,
        out_shape=jax.ShapeDtypeStruct((bands, 16, LONS // bands), BF16),
        scratch_shapes=[pltpu.VMEM((16, LONS), F32)],
        compiler_params=pltpu.CompilerParams(vmem_limit_bytes=16 << 20),
        name="grid",
    )(points, wave, own, cos, sin)


def gather_kernel(rows_ref, out_ref):
    fields = rows_ref.shape[1]
    for k in range(rows_ref.shape[0]):
        out_ref[k * fields : (k + 1) * fields, 0, :] = rows_ref[k].astype(F32)


def gather_rows(rows):
    bands, fields, width = rows.shape
    vmem = pl.BlockSpec(memory_space=pltpu.VMEM)
    return pl.pallas_call(
        gather_kernel,
        in_specs=[vmem],
        out_specs=vmem,
        out_shape=jax.ShapeDtypeStruct((bands * fields, 1, width), F32),
        compiler_params=pltpu.CompilerParams(vmem_limit_bytes=4 << 20),
        name="gather",
    )(rows)


def scale_quarters(quarter, scale_ref, line_ref):
    bands = scale_ref.shape[0]
    tiles = LONS // (128 * bands)
    for k in range(bands):
        for i in range(tiles):
            at = 128 * (k * tiles + i)
            line_ref[:, at : at + 128] = jnp.broadcast_to(scale_ref[k, i : i + 1, :], (8, 128))
    keep = lax.broadcasted_iota(jnp.int32, (8, QPAD), 1) < quarter
    wide = QPAD + 128
    parts = []
    for t in range(4):
        first = quarter * t
        part = line_ref[:, pl.ds(pl.multiple_of((first >> 7) * 128, 128), wide)]
        part = pltpu.roll(part, lax.rem(wide - (first & 127), wide), 1)
        parts.append(jnp.where(keep, part[:, :QPAD], 0.0)[0:1])
    return parts


def back_kernel(
    points_ref, band_ref, wave_ref, own_ref, other_ref, mix_ref, scale_ref, cos_ref, sin_ref, out_ref, line_ref
):
    points_int = points_ref[0]
    quarter = points_int >> 2
    low = (band_ref[0] & 1) == 0
    wave = wave_ref[...]
    own = coefficients(own_ref[...])
    other = coefficients(other_ref[...])
    mix = jnp.where(low, mix_ref[0:16, :], mix_ref[16:32, :])
    high = mix.astype(BF16)
    rest = mix - high.astype(F32)
    middle = rest.astype(BF16)
    last = (rest - middle.astype(F32)).astype(BF16)
    factors = jnp.concatenate([high.astype(F32), middle.astype(F32), last.astype(F32)], axis=0).astype(BF16)
    mixed = []
    for mine, its in zip(own, other):
        levels = jnp.concatenate([jnp.where(low, mine, its), jnp.where(low, its, mine)], axis=0).astype(BF16)
        terms = jnp.dot(factors, levels, preferred_element_type=F32)
        mixed.append(terms[0:16] + terms[16:32] + terms[32:48])
    quarters = inverse_quarters(mixed[0], mixed[1], wave, points_int, cos_ref, sin_ref)
    scales = scale_quarters(quarter, scale_ref, line_ref)
    q0, q1, q2, q3 = (part * scale for part, scale in zip(quarters, scales))
    even = q0 + q2
    odds = q1 + q3
    folded = jnp.concatenate([even + odds, even - odds, q0 - q2, q1 - q3], axis=0).astype(BF16)
    by_cos = lax.dot_general(folded, cos_ref[...], NT, preferred_element_type=F32)
    by_sin = lax.dot_general(folded, sin_ref[...], NT, preferred_element_type=F32)
    inverse = 1.0 / jnp.full((1, KPAD), points_int, jnp.int32).astype(F32)
    v0, v1, v2, v3 = classes(wave, points_int, inverse)
    odd = v1 + v3
    cosines = by_cos[0:16] * v0 + by_cos[16:32] * v2 + by_cos[32:48] * odd + by_sin[48:64] * (v3 - v1)
    sines = by_sin[0:16] * v0 + by_sin[16:32] * v2 + by_sin[32:48] * odd + by_cos[48:64] * (v1 - v3)
    width = LAT * ROWS
    rows = []
    for k in range(GROUP):
        rows.append(cosines[:, k * width : (k + 1) * width])
        rows.append(-sines[:, k * width : (k + 1) * width])
    rows.append(jnp.zeros((128 - 32 * GROUP, width), F32))
    out_ref[...] = jnp.concatenate(rows, axis=0).T.astype(BF16)


def back_rows(points, band, wave, own, other, mix, scale, cos, sin):
    vmem = pl.BlockSpec(memory_space=pltpu.VMEM)
    smem = pl.BlockSpec(memory_space=pltpu.SMEM)
    return pl.pallas_call(
        back_kernel,
        in_specs=[smem, smem] + [vmem] * 7,
        out_specs=vmem,
        out_shape=jax.ShapeDtypeStruct((LAT * ROWS, 128), BF16),
        scratch_shapes=[pltpu.VMEM((8, LONS), F32)],
        compiler_params=pltpu.CompilerParams(vmem_limit_bytes=16 << 20),
        name="back",
    )(points, band, wave, own, other, mix, scale, cos, sin)


def body(spectral, legendre, slot_wave, lat_points, level_mix, grid_scale, gauss_w):
    slots = spectral.shape[0]
    bands = lax.axis_size("band")
    base = (lax.axis_index("wave") * slots).astype(jnp.int32)[None]
    band = lax.axis_index("band").astype(jnp.int32)[None]

    width = grid_scale.shape[1]

    scale = jnp.pad(grid_scale.reshape(1, width // 128, 128), ((0, 0), (0, 8 - width // 128), (0, 0)))
    scale = lax.all_to_all(jnp.broadcast_to(scale, (bands, 8, 128)), "band", 0, 0, tiled=True)
    four = legendre_inverse(base, slot_wave, spectral, legendre)

    by_row = jnp.pad(slot_wave.reshape(LAT, ROWS - 1, GROUP), ((0, 0), (0, 1), (0, 0)), constant_values=M)
    wave = jnp.transpose(by_row, (2, 0, 1)).reshape(1, KPAD)
    wave_rows = wave.reshape(KPAD // 128, 128).astype(F32)

    four, scale, wave, wave_rows, band = lax.optimization_barrier((four, scale, wave, wave_rows, band))
    message = lax.all_to_all(four.reshape(LAT, ROWS, 128), "wave", 0, 0, tiled=True)
    own, points = lax.optimization_barrier((message.reshape(LAT * ROWS, 128), lat_points))
    other = lax.ppermute(own, "band", [(k, k ^ 1) for k in range(bands)])
    cos, sin = trig_tables(points, wave_rows)
    rows = grid_rows(points, wave, own, cos, sin, bands)
    back = back_rows(points, band, wave, own, other, level_mix, scale, cos, sin)
    back = lax.all_to_all(back.reshape(LAT, ROWS, 128), "wave", 0, 0, tiled=True)
    rows, back = lax.optimization_barrier((rows, back))
    rows = lax.all_to_all(rows, "band", 0, 0, tiled=True)
    spec_out = legendre_direct(base, slot_wave, back.reshape(LAT * ROWS, 128), legendre, gauss_w)
    return gather_rows(rows), spec_out.reshape(spectral.shape)


def solution(mesh):
    placed = (
        P("wave", None, "band", None),
        P("wave", None, None),
        P(),
        P("wave"),
        P(),
        P("wave", "band"),
        P(),
    )

    return jax.shard_map(
        body,
        mesh=mesh,
        in_specs=placed,
        out_specs=(P(None, "wave", "band"), P("wave", None, "band", None)),
        check_vma=False,
    )
```

time: 279 us -> 110 us (0.39)
  other arithmetic: 84.5 us -> 0.71 us
  blocking collectives: 76.9 us -> 36.1 us
  matrix products: 33.7 us -> 0 us
  starting transfers between devices: 50.8 us -> 22.5 us
  Pallas kernels: 0 us -> 27.6 us
  local copies, waits for them, and re-layouts: 16.8 us -> 7.85 us
    another operation x1 -> x0, other arithmetic: 84.3 us -> none  [trig_table(): return jnp.stack([jnp.cos(angle_rad), jnp.sin(angle_rad)], axis=2)]
    unnamed x1 -> x0, blocking collectives: 53.6 us -> none
    all_to_all x0 -> x1, blocking collectives: none -> 36.1 us  [body(): lax.all_to_all(four.reshape(LAT, ROWS, 128), 'wave', 0, 0, tiled=True)]
    dot_general x5 -> x0, matrix products: 33.7 us -> none  [the longest x1 12.6 us: inverse_terms(): jnp.einsum('scfa,ascj->faj', weighted, trig_tab, precision=lax.Precision....]
    all_to_all x2 -> x3, starting transfers between devices: 50.8 us -> 19.2 us  [the longest x1 7.64 us: body(): lax.all_to_all(jnp.broadcast_to(scale, (bands, 8, 128)), 'band', 0, 0, ti...]
    pallas_call x0 -> x6, Pallas kernels: none -> 27.6 us  [the longest x1 7.12 us: back_rows(): pl.pallas_call(back_kernel, in_specs=[smem, smem] + [vmem] * 7, out_specs...]
    all_gather x1 -> x0, blocking collectives: 23.3 us -> none  [body(): lax.all_gather(fourier, 'band', axis=2, tiled=True)]
    ppermute x0 -> x1, starting transfers between devices: none -> 3.3 us  [body(): other = lax.ppermute(own, 'band', [(k, k ^ 1) for k in range(bands)])]
  transfers between devices with their start and end apart: 2 -> 4, of which waited for: 1 -> 2; matrix products, arithmetic and copies ran while one was open for 31% -> 1% of each run, Pallas kernels for 0% -> 18%
where the time goes in v1:
time: 110 us; the launch traced here: 109 us
  blocking collectives  36.1 us (33%)
  Pallas kernels  27.6 us (25%)
  starting transfers between devices  22.5 us (20%)
  waiting for transfers between devices  12.8 us (12%)
  local copies, waits for them, and re-layouts  7.85 us (7%)
  between operations  1.44 us (1%)
    all_to_all x1, blocking collectives, body(): lax.all_to_all(four.reshape(LAT, ROWS, 128), 'wave', 0, 0, tiled=True)  36.1 us
    all_to_all x1, waiting for transfers between devices, body(): lax.all_to_all(back.reshape(LAT, ROWS, 128), 'wave', 0, 0, tiled=True)  7.9 us
    all_to_all x1, starting transfers between devices, body(): lax.all_to_all(jnp.broadcast_to(scale, (bands, 8, 128)), 'band', 0, 0, ti...  7.64 us
    pallas_call x1, Pallas kernels, back_rows(): pl.pallas_call(back_kernel, in_specs=[smem, smem] + [vmem] * 7, out_specs...  7.12 us
    all_to_all x1, starting transfers between devices, body(): lax.all_to_all(back.reshape(LAT, ROWS, 128), 'wave', 0, 0, tiled=True)  6.06 us
    pallas_call x1, Pallas kernels, legendre_inverse(): pl.pallas_call(legendre_inverse_kernel, in_specs=[smem, smem, hbm, hbm],...  6.05 us
    pallas_call x1, Pallas kernels, trig_tables(): pl.pallas_call(table_kernel, in_specs=[pl.BlockSpec(memory_space=pltpu.SM...  5.96 us
    unnamed x12, local copies, waits for them, and re-layouts  5.69 us
  transfers between devices with their start and end apart: 4, of which 2 were waited for; matrix products, arithmetic and copies ran while one was open for 1% of the time, Pallas kernels for 18%

profile of v1, /device:TPU:1, one launch (start us, length us, event | category | flops | bytes accessed | tf_op | source)
XLA Modules:
  0.0 109.0 jit_solution(12294153917831902469)
XLA Ops:
  0.6 0.0 copy-start.4
  0.6 0.7 reduce
  1.4 0.6 broadcast_in_dim.18
  2.0 7.6 %all-to-all-start = ((f32[8,8,128]{2,1,0:T(8,128)}), f32[8,8,128]{2,1,0:T(8,128)S(1)}, u32[]{:S(2)}, u32[]{:S(2)}) async-start(f32[8,8,128]{2,1,0:T(8,128)} %broadcast_in_dim.18), calls=%async_computation | async-start | bytes 65536 | tf_op jit(solution)/shard_map/all_to_all | solution.py:372
  9.6 0.9 reshape.34
  10.5 0.2 copy.11
  10.7 0.1 copy.13
  10.8 0.1 convert_element_type.9.wave_ref
  11.0 0.1 copy.12
  11.1 0.1 reshape.35.wave_ref
  11.2 6.1 %legendre_inverse.1 = bf16[768,128]{1,0:T(8,128)(2,1)} custom-call(s32[1]{0:T(128)} %bitcast.base_ref, s32[2016]{0:T(1024)} %wave_ref.3, bf16[21,32,1280]{2,1,0:T(8,128)(2,1)} %bitcast.19, bf16[21,96,1280]{2,1,0:T(8,128)(2,1)} %leg_ref.3), custom_call_target="tpu_custom_call" | custom-call | tf_op jit(solution)/shard_map/legendre_inverse/pallas_call | solution.py:62
  17.3 0.0 all-to-all-done.scale_ref
  17.3 36.1 %all_to_all.20 = bf16[96,8,128]{2,1,0:T(8,128)(2,1)S(1)} all-to-all(bf16[96,8,128]{2,1,0:T(8,128)(2,1)} %bitcast.22), channel_id=1, replica_groups=mesh['wave'=96,'band'=8] {'wave'}, dimensions={0} | all-to-all | bytes 393216 | tf_op jit(solution)/shard_map/all_to_all | solution.py:380
  53.4 3.3 %collective-permute-start = (bf16[768,128]{1,0:T(8,128)(2,1)S(1)}, bf16[768,128]{1,0:T(8,128)(2,1)S(1)}, u32[]{:S(2)}, u32[]{:S(2)}) collective-permute-start(bf16[768,128]{1,0:T(8,128)(2,1)S(1)} %bitcast.16), channel_id=1, source_target_pairs={{0,1},{1,0},{2,3},{3,2},{4,5},{5,4},{6,7},{7,6},{8,9},{9,8},{10,11... | collective-permute-start | bytes 589832 | tf_op jit(solution)/shard_map/ppermute | solution.py:382
  57.3 6.0 %tables.1 = (bf16[2304,1408]{1,0:T(8,128)(2,1)S(1)}, bf16[2304,1408]{1,0:T(8,128)(2,1)S(1)}) custom-call(s32[1]{0:T(128)S(6)} %copy.14.points_ref, f32[18,128]{1,0:T(8,128)S(1)} %convert_element_type.9.wave_ref), custom_call_target="tpu_custom_call" | custom-call | tf_op jit(solution)/shard_map/tables/pallas_call | solution.py:193
  63.3 0.0 copy-start
  63.3 0.0 copy-start.2
  63.3 0.0 collective-permute-done.other_ref
  63.3 0.0 copy-done.4
  63.4 7.1 %back.1 = bf16[768,128]{1,0:T(8,128)(2,1)} custom-call(s32[1]{0:T(128)S(6)} %copy.14.points_ref, s32[1]{0:T(128)} %bitcast.4.band_ref, s32[1,2304]{1,0:T(1,128)S(1)} %reshape.35.wave_ref, bf16[768,128]{1,0:T(8,128)(2,1)S(1)} %bitcast.17, bf16[768,128]{1,0:T(8,128)(2,1)S(1)} %collective-permute-done.other_ref, f32[32,32]{1,0:T(8,128)S(1)} %copy-done.4, ...), custom_call_target="tpu_custom_call" | custom-call | tf_op jit(solution)/shard_map/back/pallas_call | solution.py:352
  70.5 0.0 copy-done
  70.5 0.0 copy-done.2
  70.5 6.1 %all-to-all-start.2 = ((bf16[96,8,128]{2,1,0:T(8,128)(2,1)}), bf16[96,8,128]{2,1,0:T(8,128)(2,1)S(1)}, u32[]{:S(2)}, u32[]{:S(2)}) async-start(bf16[96,8,128]{2,1,0:T(8,128)(2,1)} %bitcast.7), calls=%async_computation.2 | async-start | bytes 393216 | tf_op jit(solution)/shard_map/all_to_all | solution.py:386
  76.5 0.0 copy-start.1
  76.6 2.8 %copy-done.1 = bf16[2304,1408]{1,0:T(8,128)(2,1)S(1)} copy-done((bf16[2304,1408]{1,0:T(8,128)(2,1)S(1)}, bf16[2304,1408]{1,0:T(8,128)(2,1)}, u32[]{:S(2)}) %copy-start.1) | copy-done | bytes 6488088
  79.4 0.0 copy-start.3
  79.4 2.8 %copy-done.3 = bf16[2304,1408]{1,0:T(8,128)(2,1)S(1)} copy-done((bf16[2304,1408]{1,0:T(8,128)(2,1)S(1)}, bf16[2304,1408]{1,0:T(8,128)(2,1)}, u32[]{:S(2)}) %copy-start.3) | copy-done | bytes 6488088
  82.2 3.1 %grid.1 = bf16[8,16,768]{2,1,0:T(8,128)(2,1)} custom-call(s32[1]{0:T(128)S(6)} %copy.14.points_ref, s32[1,2304]{1,0:T(1,128)S(1)} %reshape.35.wave_ref, bf16[768,128]{1,0:T(8,128)(2,1)S(1)} %bitcast.18, bf16[2304,1408]{1,0:T(8,128)(2,1)S(1)} %copy-done.1, bf16[2304,1408]{1,0:T(8,128)(2,1)S(1)} %copy-done.3), custom_call_target="tpu_custom_call" | custom-call | tf_op jit(solution)/shard_map/grid/pallas_call | solution.py:259
  85.3 7.9 %all-to-all-done.2 = bf16[96,8,128]{2,1,0:T(8,128)(2,1)S(1)} async-done(((bf16[96,8,128]{2,1,0:T(8,128)(2,1)}), bf16[96,8,128]{2,1,0:T(8,128)(2,1)S(1)}, u32[]{:S(2)}, u32[]{:S(2)}) %all-to-all-start.2) | async-done | bytes 196640 | tf_op jit(solution)/shard_map/all_to_all | solution.py:386
  93.2 0.0 copy-start.5
  93.2 5.5 %all-to-all-start.3 = ((bf16[8,16,768]{2,1,0:T(8,128)(2,1)}), bf16[8,16,768]{2,1,0:T(8,128)(2,1)S(1)}, u32[]{:S(2)}, u32[]{:S(2)}) async-start(bf16[8,16,768]{2,1,0:T(8,128)(2,1)} %grid.1), calls=%async_computation.3 | async-start | bytes 393216 | tf_op jit(solution)/shard_map/all_to_all | solution.py:388
  98.7 0.0 copy-done.5
  98.7 4.6 %legendre_direct.1 = bf16[21,32,1280]{2,1,0:T(8,128)(2,1)} custom-call(s32[1]{0:T(128)} %bitcast.base_ref, s32[2016]{0:T(1024)} %wave_ref.3, bf16[768,128]{1,0:T(8,128)(2,1)} %bitcast.21, bf16[21,96,1280]{2,1,0:T(8,128)(2,1)} %leg_ref.3, f32[1,96]{1,0:T(1,128)} %bitcast.24), custom_call_target="tpu_custom_call" | custom-call | tf_op jit(solution)/shard_map/legendre_direct/pallas_call | solution.py:109
  103.3 4.9 %all-to-all-done.3.rows_ref = bf16[8,16,768]{2,1,0:T(8,128)(2,1)S(1)} async-done(((bf16[8,16,768]{2,1,0:T(8,128)(2,1)}), bf16[8,16,768]{2,1,0:T(8,128)(2,1)S(1)}, u32[]{:S(2)}, u32[]{:S(2)}) %all-to-all-start.3) | async-done | bytes 196640 | tf_op jit(solution)/shard_map/all_to_all | solution.py:388
  108.2 0.8 gather.1
  (2 shorter events, 0.0 us)
Async XLA Ops:
  0.6 62.7 %copy-start.4 = (f32[32,32]{1,0:T(8,128)S(1)}, f32[32,32]{1,0:T(8,128)}, u32[]{:S(2)}) copy-start(f32[32,32]{1,0:T(8,128)} %mix_ref.1) | copy-start | bytes 12292
  2.0 15.3 %all-to-all-start = ((f32[8,8,128]{2,1,0:T(8,128)}), f32[8,8,128]{2,1,0:T(8,128)S(1)}, u32[]{:S(2)}, u32[]{:S(2)}) async-start(f32[8,8,128]{2,1,0:T(8,128)} %broadcast_in_dim.18), calls=%async_computation | async-start | bytes 65536 | tf_op jit(solution)/shard_map/all_to_all | solution.py:372
  53.4 9.9 %collective-permute-start = (bf16[768,128]{1,0:T(8,128)(2,1)S(1)}, bf16[768,128]{1,0:T(8,128)(2,1)S(1)}, u32[]{:S(2)}, u32[]{:S(2)}) collective-permute-start(bf16[768,128]{1,0:T(8,128)(2,1)S(1)} %bitcast.16), channel_id=1, source_target_pairs={{0,1},{1,0},{2,3},{3,2},{4,5},{5,4},{6,7},{7,6},{8,9},{9,8},{10,11... | collective-permute-start | bytes 589832 | tf_op jit(solution)/shard_map/ppermute | solution.py:382
  63.3 7.2 %copy-start = (bf16[2304,1408]{1,0:T(8,128)(2,1)}, bf16[2304,1408]{1,0:T(8,128)(2,1)S(1)}, u32[]{:S(2)}) copy-start(bf16[2304,1408]{1,0:T(8,128)(2,1)S(1)} %get-tuple-element.18.cos_ref) | copy-start | bytes 19464196
  63.3 7.2 %copy-start.2 = (bf16[2304,1408]{1,0:T(8,128)(2,1)}, bf16[2304,1408]{1,0:T(8,128)(2,1)S(1)}, u32[]{:S(2)}) copy-start(bf16[2304,1408]{1,0:T(8,128)(2,1)S(1)} %get-tuple-element.19.sin_ref) | copy-start | bytes 19464196
  70.5 22.7 %all-to-all-start.2 = ((bf16[96,8,128]{2,1,0:T(8,128)(2,1)}), bf16[96,8,128]{2,1,0:T(8,128)(2,1)S(1)}, u32[]{:S(2)}, u32[]{:S(2)}) async-start(bf16[96,8,128]{2,1,0:T(8,128)(2,1)} %bitcast.7), calls=%async_computation.2 | async-start | bytes 393216 | tf_op jit(solution)/shard_map/all_to_all | solution.py:386
  76.5 2.8 %copy-start.1 = (bf16[2304,1408]{1,0:T(8,128)(2,1)S(1)}, bf16[2304,1408]{1,0:T(8,128)(2,1)}, u32[]{:S(2)}) copy-start(bf16[2304,1408]{1,0:T(8,128)(2,1)} %copy-done) | copy-start | bytes 19464196
  79.4 2.8 %copy-start.3 = (bf16[2304,1408]{1,0:T(8,128)(2,1)S(1)}, bf16[2304,1408]{1,0:T(8,128)(2,1)}, u32[]{:S(2)}) copy-start(bf16[2304,1408]{1,0:T(8,128)(2,1)} %copy-done.2) | copy-start | bytes 19464196
  93.2 5.5 %copy-start.5 = (bf16[96,8,128]{2,1,0:T(8,128)(2,1)}, bf16[96,8,128]{2,1,0:T(8,128)(2,1)S(1)}, u32[]{:S(2)}) copy-start(bf16[96,8,128]{2,1,0:T(8,128)(2,1)S(1)} %all-to-all-done.2) | copy-start | bytes 589828
  93.2 15.0 %all-to-all-start.3 = ((bf16[8,16,768]{2,1,0:T(8,128)(2,1)}), bf16[8,16,768]{2,1,0:T(8,128)(2,1)S(1)}, u32[]{:S(2)}, u32[]{:S(2)}) async-start(bf16[8,16,768]{2,1,0:T(8,128)(2,1)} %grid.1), calls=%async_computation.3 | async-start | bytes 393216 | tf_op jit(solution)/shard_map/all_to_all | solution.py:388

commit v2 on v1

--- a/solution.py
+++ b/solution.py
@@ -286,13 +286,11 @@
     )(rows)
 
 
-def scale_quarters(quarter, scale_ref, line_ref):
-    bands = scale_ref.shape[0]
-    tiles = LONS // (128 * bands)
+def scale_quarters(band, quarter, scale_ref, line_ref):
+    bands, width = scale_ref.shape
     for k in range(bands):
-        for i in range(tiles):
-            at = 128 * (k * tiles + i)
-            line_ref[:, at : at + 128] = jnp.broadcast_to(scale_ref[k, i : i + 1, :], (8, 128))
+        row = scale_ref[pl.ds(band ^ k, 1), :]
+        line_ref[:, k * width : (k + 1) * width] = jnp.broadcast_to(row, (8, width))
     keep = lax.broadcasted_iota(jnp.int32, (8, QPAD), 1) < quarter
     wide = QPAD + 128
     parts = []
@@ -325,7 +323,7 @@
         terms = jnp.dot(factors, levels, preferred_element_type=F32)
         mixed.append(terms[0:16] + terms[16:32] + terms[32:48])
     quarters = inverse_quarters(mixed[0], mixed[1], wave, points_int, cos_ref, sin_ref)
-    scales = scale_quarters(quarter, scale_ref, line_ref)
+    scales = scale_quarters(band_ref[0], quarter, scale_ref, line_ref)
     q0, q1, q2, q3 = (part * scale for part, scale in zip(quarters, scales))
     even = q0 + q2
     odds = q1 + q3
@@ -366,20 +364,25 @@
     base = (lax.axis_index("wave") * slots).astype(jnp.int32)[None]
     band = lax.axis_index("band").astype(jnp.int32)[None]
 
-    width = grid_scale.shape[1]
-
-    scale = jnp.pad(grid_scale.reshape(1, width // 128, 128), ((0, 0), (0, 8 - width // 128), (0, 0)))
-    scale = lax.all_to_all(jnp.broadcast_to(scale, (bands, 8, 128)), "band", 0, 0, tiled=True)
+
+    def swap(array, k):
+        return lax.ppermute(array, "band", [(i, i ^ k) for i in range(bands)])
+
     four = legendre_inverse(base, slot_wave, spectral, legendre)
+    message = lax.all_to_all(four.reshape(LAT, ROWS, 128), "wave", 0, 0, tiled=True)
+
+    scale = grid_scale
+    for k in (1, 2, 4):
+        scale = jnp.concatenate([scale, swap(scale, k)], axis=0)
 
     by_row = jnp.pad(slot_wave.reshape(LAT, ROWS - 1, GROUP), ((0, 0), (0, 1), (0, 0)), constant_values=M)
     wave = jnp.transpose(by_row, (2, 0, 1)).reshape(1, KPAD)
     wave_rows = wave.reshape(KPAD // 128, 128).astype(F32)
 
-    four, scale, wave, wave_rows, band = lax.optimization_barrier((four, scale, wave, wave_rows, band))
-    message = lax.all_to_all(four.reshape(LAT, ROWS, 128), "wave", 0, 0, tiled=True)
-    own, points = lax.optimization_barrier((message.reshape(LAT * ROWS, 128), lat_points))
-    other = lax.ppermute(own, "band", [(k, k ^ 1) for k in range(bands)])
+    own, scale, wave, wave_rows, points, band = lax.optimization_barrier(
+        (message.reshape(LAT * ROWS, 128), scale, wave, wave_rows, lat_points, band)
+    )
+    other = swap(own, 1)
     cos, sin = trig_tables(points, wave_rows)
     rows = grid_rows(points, wave, own, cos, sin, bands)
     back = back_rows(points, band, wave, own, other, level_mix, scale, cos, sin)

time: 110 us -> 112 us (1.018)
  starting transfers between devices: 22.5 us -> 60.2 us
  blocking collectives: 36.1 us -> 0 us
  waiting for transfers between devices: 12.8 us -> 14.9 us
  local copies, waits for them, and re-layouts: 7.85 us -> 6.54 us
    all_to_all x1 -> x0, blocking collectives: 36.1 us -> none  [body(): lax.all_to_all(four.reshape(LAT, ROWS, 128), 'wave', 0, 0, tiled=True)]
    ppermute x1 -> x4, starting transfers between devices: 3.3 us -> 17.9 us  [swap(): return lax.ppermute(array, 'band', [(i, i ^ k) for i in range(bands)])]
    all_to_all x1, starting transfers between devices: 7.64 us -> 20 us  [body(): lax.all_to_all(four.reshape(LAT, ROWS, 128), 'wave', 0, 0, tiled=True)]
    all_to_all x1, starting transfers between devices: 6.06 us -> 16.3 us  [body(): lax.all_to_all(back.reshape(LAT, ROWS, 128), 'wave', 0, 0, tiled=True)]
    ppermute x1 -> x4, waiting for transfers between devices: 0.01 us -> 2.95 us  [swap(): return lax.ppermute(array, 'band', [(i, i ^ k) for i in range(bands)])]
    unnamed x12 -> x16, local copies, waits for them, and re-layouts: 5.69 us -> 5.7 us
  transfers between devices with their start and end apart: 4 -> 7, of which waited for: 2 -> 5; matrix products, arithmetic and copies ran while one was open for 1% -> 1% of each run, Pallas kernels for 18% -> 12%
where the time goes in v2:
time: 112 us; the launch traced here: 111 us
  starting transfers between devices  60.2 us (54%)
  Pallas kernels  27.8 us (25%)
  waiting for transfers between devices  14.9 us (13%)
  local copies, waits for them, and re-layouts  6.54 us (6%)
  between operations  1.51 us (1%)
    all_to_all x1, starting transfers between devices, body(): lax.all_to_all(four.reshape(LAT, ROWS, 128), 'wave', 0, 0, tiled=True)  20 us
    ppermute x4, starting transfers between devices, swap(): return lax.ppermute(array, 'band', [(i, i ^ k) for i in range(bands)])  17.9 us
    all_to_all x1, starting transfers between devices, body(): lax.all_to_all(back.reshape(LAT, ROWS, 128), 'wave', 0, 0, tiled=True)  16.3 us
    all_to_all x1, waiting for transfers between devices, body(): lax.all_to_all(back.reshape(LAT, ROWS, 128), 'wave', 0, 0, tiled=True)  7.52 us
    pallas_call x1, Pallas kernels, back_rows(): pl.pallas_call(back_kernel, in_specs=[smem, smem] + [vmem] * 7, out_specs...  7.13 us
    pallas_call x1, Pallas kernels, legendre_inverse(): pl.pallas_call(legendre_inverse_kernel, in_specs=[smem, smem, hbm, hbm],...  6.18 us
    pallas_call x1, Pallas kernels, trig_tables(): pl.pallas_call(table_kernel, in_specs=[pl.BlockSpec(memory_space=pltpu.SM...  5.96 us
    all_to_all x1, starting transfers between devices, body(): rows = lax.all_to_all(rows, 'band', 0, 0, tiled=True)  5.92 us
  transfers between devices with their start and end apart: 7, of which 5 were waited for; matrix products, arithmetic and copies ran while one was open for 1% of the time, Pallas kernels for 12%

profile of v2, /device:TPU:1, one launch (start us, length us, event | category | flops | bytes accessed | tf_op | source)
XLA Modules:
  0.0 111.0 jit_solution(8612267241018929887)
XLA Ops:
  0.6 0.0 copy-start.6
  0.6 0.0 copy-start.7
  0.7 0.0 copy-start.4
  0.7 6.2 %legendre_inverse.1 = bf16[768,128]{1,0:T(8,128)(2,1)} custom-call(s32[1]{0:T(128)} %bitcast.base_ref, s32[2016]{0:T(1024)} %wave_ref.3, bf16[21,32,1280]{2,1,0:T(8,128)(2,1)} %bitcast.16, bf16[21,96,1280]{2,1,0:T(8,128)(2,1)} %leg_ref.3), custom_call_target="tpu_custom_call" | custom-call | tf_op jit(solution)/shard_map/legendre_inverse/pallas_call | solution.py:62
  6.9 20.0 %all-to-all-start = ((bf16[96,8,128]{2,1,0:T(8,128)(2,1)}), bf16[96,8,128]{2,1,0:T(8,128)(2,1)S(1)}, u32[]{:S(2)}, u32[]{:S(2)}) async-start(bf16[96,8,128]{2,1,0:T(8,128)(2,1)} %bitcast.18), calls=%async_computation | async-start | bytes 393216 | tf_op jit(solution)/shard_map/all_to_all | solution.py:372
  26.9 0.0 copy-done.7
  26.9 3.2 %collective-permute-start = (f32[1,768]{1,0:T(1,128)S(1)}, f32[1,768]{1,0:T(1,128)S(1)}, u32[]{:S(2)}, u32[]{:S(2)}) collective-permute-start(f32[1,768]{1,0:T(1,128)S(1)} %copy-done.7), channel_id=1, source_target_pairs={{0,1},{1,0},{2,3},{3,2},{4,5},{5,4},{6,7},{7,6},{8,9},{9,8},{10,11... | collective-permute-start | bytes 9224 | tf_op jit(solution)/shard_map/ppermute | solution.py:369
  30.1 1.4 %collective-permute-done = f32[1,768]{1,0:T(1,128)S(1)} collective-permute-done((f32[1,768]{1,0:T(1,128)S(1)}, f32[1,768]{1,0:T(1,128)S(1)}, u32[]{:S(2)}, u32[]{:S(2)}) %collective-permute-start) | collective-permute-done | bytes 3104 | tf_op jit(solution)/shard_map/ppermute | solution.py:369
  31.6 4.2 %collective-permute-start.1 = (f32[2,768]{1,0:T(2,128)S(1)}, f32[2,768]{1,0:T(2,128)S(1)}, u32[]{:S(2)}, u32[]{:S(2)}) collective-permute-start(f32[2,768]{1,0:T(2,128)S(1)} %pad_maximum_fusion.2), channel_id=1, source_target_pairs={{0,2},{1,3},{2,0},{3,1},{4,6},{5,7},{6,4},{7,5},{8,10},{9,11},{10,... | collective-permute-start | bytes 18440 | tf_op jit(solution)/shard_map/ppermute | solution.py:369
  35.8 0.0 copy-done.6
  35.8 0.2 reshape.32
  36.0 0.2 copy.11
  36.2 1.0 collective-permute-done.1
  37.1 7.5 %collective-permute-start.2 = (f32[4,768]{1,0:T(4,128)S(1)}, f32[4,768]{1,0:T(4,128)S(1)}, u32[]{:S(2)}, u32[]{:S(2)}) collective-permute-start(f32[4,768]{1,0:T(4,128)S(1)} %pad_maximum_fusion.1), channel_id=1, source_target_pairs={{0,4},{1,5},{2,6},{3,7},{4,0},{5,1},{6,2},{7,3},{8,12},{9,13},{10,... | collective-permute-start | bytes 36872 | tf_op jit(solution)/shard_map/ppermute | solution.py:369
  44.6 0.1 copy.13
  44.7 0.1 convert_element_type.7.wave_ref
  44.9 0.1 copy.12
  45.0 0.1 reshape.33.wave_ref
  45.1 0.6 collective-permute-done.2
  45.7 0.0 all-to-all-done
  45.7 3.0 %collective-permute-start.3 = (bf16[768,128]{1,0:T(8,128)(2,1)S(1)}, bf16[768,128]{1,0:T(8,128)(2,1)S(1)}, u32[]{:S(2)}, u32[]{:S(2)}) collective-permute-start(bf16[768,128]{1,0:T(8,128)(2,1)S(1)} %bitcast.13), channel_id=1, source_target_pairs={{0,1},{1,0},{2,3},{3,2},{4,5},{5,4},{6,7},{7,6},{8,9},{9,8},{10,11... | collective-permute-start | bytes 589832 | tf_op jit(solution)/shard_map/ppermute | solution.py:369
  49.4 6.0 %tables.1 = (bf16[2304,1408]{1,0:T(8,128)(2,1)S(1)}, bf16[2304,1408]{1,0:T(8,128)(2,1)S(1)}) custom-call(s32[1]{0:T(128)S(6)} %copy.14.points_ref, f32[18,128]{1,0:T(8,128)S(1)} %convert_element_type.7.wave_ref), custom_call_target="tpu_custom_call" | custom-call | tf_op jit(solution)/shard_map/tables/pallas_call | solution.py:193
  55.4 0.0 copy-start
  55.4 0.0 copy-start.2
  55.4 0.0 collective-permute-done.3.other_ref
  55.4 0.0 copy-done.4
  55.4 7.1 %back.1 = bf16[768,128]{1,0:T(8,128)(2,1)} custom-call(s32[1]{0:T(128)S(6)} %copy.14.points_ref, s32[1]{0:T(128)} %bitcast.5.band_ref, s32[1,2304]{1,0:T(1,128)S(1)} %reshape.33.wave_ref, bf16[768,128]{1,0:T(8,128)(2,1)S(1)} %bitcast.14, bf16[768,128]{1,0:T(8,128)(2,1)S(1)} %collective-permute-done.3.other_ref, f32[32,32]{1,0:T(8,128)S(1)} %copy-done.4, ...), custom_call_target="tpu_custom_call" | custom-call | tf_op jit(solution)/shard_map/back/pallas_call | solution.py:350
  62.5 0.0 copy-done
  62.5 0.0 copy-done.2
  62.5 16.3 %all-to-all-start.1 = ((bf16[96,8,128]{2,1,0:T(8,128)(2,1)}), bf16[96,8,128]{2,1,0:T(8,128)(2,1)S(1)}, u32[]{:S(2)}, u32[]{:S(2)}) async-start(bf16[96,8,128]{2,1,0:T(8,128)(2,1)} %bitcast.6), calls=%async_computation.1 | async-start | bytes 393216 | tf_op jit(solution)/shard_map/all_to_all | solution.py:389
  78.9 0.0 copy-start.1
  78.9 2.8 %copy-done.1 = bf16[2304,1408]{1,0:T(8,128)(2,1)S(1)} copy-done((bf16[2304,1408]{1,0:T(8,128)(2,1)S(1)}, bf16[2304,1408]{1,0:T(8,128)(2,1)}, u32[]{:S(2)}) %copy-start.1) | copy-done | bytes 6488088
  81.7 0.0 copy-start.3
  81.7 2.8 %copy-done.3 = bf16[2304,1408]{1,0:T(8,128)(2,1)S(1)} copy-done((bf16[2304,1408]{1,0:T(8,128)(2,1)S(1)}, bf16[2304,1408]{1,0:T(8,128)(2,1)}, u32[]{:S(2)}) %copy-start.3) | copy-done | bytes 6488088
  84.6 3.1 %grid.1 = bf16[8,16,768]{2,1,0:T(8,128)(2,1)} custom-call(s32[1]{0:T(128)S(6)} %copy.14.points_ref, s32[1,2304]{1,0:T(1,128)S(1)} %reshape.33.wave_ref, bf16[768,128]{1,0:T(8,128)(2,1)S(1)} %bitcast.15, bf16[2304,1408]{1,0:T(8,128)(2,1)S(1)} %copy-done.1, bf16[2304,1408]{1,0:T(8,128)(2,1)S(1)} %copy-done.3), custom_call_target="tpu_custom_call" | custom-call | tf_op jit(solution)/shard_map/grid/pallas_call | solution.py:259
  87.6 7.5 %all-to-all-done.1 = bf16[96,8,128]{2,1,0:T(8,128)(2,1)S(1)} async-done(((bf16[96,8,128]{2,1,0:T(8,128)(2,1)}), bf16[96,8,128]{2,1,0:T(8,128)(2,1)S(1)}, u32[]{:S(2)}, u32[]{:S(2)}) %all-to-all-start.1) | async-done | bytes 196640 | tf_op jit(solution)/shard_map/all_to_all | solution.py:389
  95.1 0.0 copy-start.5
  95.1 5.9 %all-to-all-start.2 = ((bf16[8,16,768]{2,1,0:T(8,128)(2,1)}), bf16[8,16,768]{2,1,0:T(8,128)(2,1)S(1)}, u32[]{:S(2)}, u32[]{:S(2)}) async-start(bf16[8,16,768]{2,1,0:T(8,128)(2,1)} %grid.1), calls=%async_computation.2 | async-start | bytes 393216 | tf_op jit(solution)/shard_map/all_to_all | solution.py:391
  101.1 0.0 copy-done.5
  101.1 4.6 %legendre_direct.1 = bf16[21,32,1280]{2,1,0:T(8,128)(2,1)} custom-call(s32[1]{0:T(128)} %bitcast.base_ref, s32[2016]{0:T(1024)} %wave_ref.3, bf16[768,128]{1,0:T(8,128)(2,1)} %bitcast.19, bf16[21,96,1280]{2,1,0:T(8,128)(2,1)} %leg_ref.3, f32[1,96]{1,0:T(1,128)} %bitcast.20), custom_call_target="tpu_custom_call" | custom-call | tf_op jit(solution)/shard_map/legendre_direct/pallas_call | solution.py:109
  105.7 4.5 %all-to-all-done.2.rows_ref = bf16[8,16,768]{2,1,0:T(8,128)(2,1)S(1)} async-done(((bf16[8,16,768]{2,1,0:T(8,128)(2,1)}), bf16[8,16,768]{2,1,0:T(8,128)(2,1)S(1)}, u32[]{:S(2)}, u32[]{:S(2)}) %all-to-all-start.2) | async-done | bytes 196640 | tf_op jit(solution)/shard_map/all_to_all | solution.py:391
  110.1 0.8 gather.1
  (4 shorter events, 0.0 us)
Async XLA Ops:
  0.6 35.1 %copy-start.6 = (s32[2016]{0:T(1024)S(1)}, s32[2016]{0:T(1024)}, u32[]{:S(2)}) copy-start(s32[2016]{0:T(1024)} %wave_ref.3) | copy-start | bytes 24196
  0.6 26.3 %copy-start.7 = (f32[1,768]{1,0:T(1,128)S(1)}, f32[1,768]{1,0:T(1,128)}, u32[]{:S(2)}) copy-start(f32[1,768]{1,0:T(1,128)} %param.12) | copy-start | bytes 9220
  0.7 54.7 %copy-start.4 = (f32[32,32]{1,0:T(8,128)S(1)}, f32[32,32]{1,0:T(8,128)}, u32[]{:S(2)}) copy-start(f32[32,32]{1,0:T(8,128)} %mix_ref.1) | copy-start | bytes 12292
  6.9 38.8 %all-to-all-start = ((bf16[96,8,128]{2,1,0:T(8,128)(2,1)}), bf16[96,8,128]{2,1,0:T(8,128)(2,1)S(1)}, u32[]{:S(2)}, u32[]{:S(2)}) async-start(bf16[96,8,128]{2,1,0:T(8,128)(2,1)} %bitcast.18), calls=%async_computation | async-start | bytes 393216 | tf_op jit(solution)/shard_map/all_to_all | solution.py:372
  26.9 4.6 %collective-permute-start = (f32[1,768]{1,0:T(1,128)S(1)}, f32[1,768]{1,0:T(1,128)S(1)}, u32[]{:S(2)}, u32[]{:S(2)}) collective-permute-start(f32[1,768]{1,0:T(1,128)S(1)} %copy-done.7), channel_id=1, source_target_pairs={{0,1},{1,0},{2,3},{3,2},{4,5},{5,4},{6,7},{7,6},{8,9},{9,8},{10,11... | collective-permute-start | bytes 9224 | tf_op jit(solution)/shard_map/ppermute | solution.py:369
  31.6 5.6 %collective-permute-start.1 = (f32[2,768]{1,0:T(2,128)S(1)}, f32[2,768]{1,0:T(2,128)S(1)}, u32[]{:S(2)}, u32[]{:S(2)}) collective-permute-start(f32[2,768]{1,0:T(2,128)S(1)} %pad_maximum_fusion.2), channel_id=1, source_target_pairs={{0,2},{1,3},{2,0},{3,1},{4,6},{5,7},{6,4},{7,5},{8,10},{9,11},{10,... | collective-permute-start | bytes 18440 | tf_op jit(solution)/shard_map/ppermute | solution.py:369
  37.1 8.5 %collective-permute-start.2 = (f32[4,768]{1,0:T(4,128)S(1)}, f32[4,768]{1,0:T(4,128)S(1)}, u32[]{:S(2)}, u32[]{:S(2)}) collective-permute-start(f32[4,768]{1,0:T(4,128)S(1)} %pad_maximum_fusion.1), channel_id=1, source_target_pairs={{0,4},{1,5},{2,6},{3,7},{4,0},{5,1},{6,2},{7,3},{8,12},{9,13},{10,... | collective-permute-start | bytes 36872 | tf_op jit(solution)/shard_map/ppermute | solution.py:369
  45.7 9.7 %collective-permute-start.3 = (bf16[768,128]{1,0:T(8,128)(2,1)S(1)}, bf16[768,128]{1,0:T(8,128)(2,1)S(1)}, u32[]{:S(2)}, u32[]{:S(2)}) collective-permute-start(bf16[768,128]{1,0:T(8,128)(2,1)S(1)} %bitcast.13), channel_id=1, source_target_pairs={{0,1},{1,0},{2,3},{3,2},{4,5},{5,4},{6,7},{7,6},{8,9},{9,8},{10,11... | collective-permute-start | bytes 589832 | tf_op jit(solution)/shard_map/ppermute | solution.py:369
  55.4 7.2 %copy-start = (bf16[2304,1408]{1,0:T(8,128)(2,1)}, bf16[2304,1408]{1,0:T(8,128)(2,1)S(1)}, u32[]{:S(2)}) copy-start(bf16[2304,1408]{1,0:T(8,128)(2,1)S(1)} %get-tuple-element.16.cos_ref) | copy-start | bytes 19464196
  55.4 7.2 %copy-start.2 = (bf16[2304,1408]{1,0:T(8,128)(2,1)}, bf16[2304,1408]{1,0:T(8,128)(2,1)S(1)}, u32[]{:S(2)}) copy-start(bf16[2304,1408]{1,0:T(8,128)(2,1)S(1)} %get-tuple-element.17.sin_ref) | copy-start | bytes 19464196
  62.5 32.6 %all-to-all-start.1 = ((bf16[96,8,128]{2,1,0:T(8,128)(2,1)}), bf16[96,8,128]{2,1,0:T(8,128)(2,1)S(1)}, u32[]{:S(2)}, u32[]{:S(2)}) async-start(bf16[96,8,128]{2,1,0:T(8,128)(2,1)} %bitcast.6), calls=%async_computation.1 | async-start | bytes 393216 | tf_op jit(solution)/shard_map/all_to_all | solution.py:389
  78.9 2.8 %copy-start.1 = (bf16[2304,1408]{1,0:T(8,128)(2,1)S(1)}, bf16[2304,1408]{1,0:T(8,128)(2,1)}, u32[]{:S(2)}) copy-start(bf16[2304,1408]{1,0:T(8,128)(2,1)} %copy-done) | copy-start | bytes 19464196
  81.7 2.8 %copy-start.3 = (bf16[2304,1408]{1,0:T(8,128)(2,1)S(1)}, bf16[2304,1408]{1,0:T(8,128)(2,1)}, u32[]{:S(2)}) copy-start(bf16[2304,1408]{1,0:T(8,128)(2,1)} %copy-done.2) | copy-start | bytes 19464196
  95.1 5.9 %copy-start.5 = (bf16[96,8,128]{2,1,0:T(8,128)(2,1)}, bf16[96,8,128]{2,1,0:T(8,128)(2,1)S(1)}, u32[]{:S(2)}) copy-start(bf16[96,8,128]{2,1,0:T(8,128)(2,1)S(1)} %all-to-all-done.1) | copy-start | bytes 589828
  95.1 15.0 %all-to-all-start.2 = ((bf16[8,16,768]{2,1,0:T(8,128)(2,1)}), bf16[8,16,768]{2,1,0:T(8,128)(2,1)S(1)}, u32[]{:S(2)}, u32[]{:S(2)}) async-start(bf16[8,16,768]{2,1,0:T(8,128)(2,1)} %grid.1), calls=%async_computation.2 | async-start | bytes 393216 | tf_op jit(solution)/shard_map/all_to_all | solution.py:391
